TPU v7x, 32 devices: a whole 2x2x4 slice. The times are simulated.
32 devices in a mesh: row: 4 (over y, x), col: 2 (over core), depth: 4 (over z).
Axes of the slice: x: 2, y: 2, z: 4, core: 2. Of those that a mesh axis runs over, the one named last changes fastest.
Arguments:
- source_desc: bfloat16 [2048, 256], P(('row', 'col', 'depth')), may hold values from -4 to 4
- target_desc: bfloat16 [16384, 256], P(('col', 'depth', 'row')), may hold values from -4 to 4
- target_dual: float32 [16384], P(('col', 'depth')), may hold values from -2 to 4.25
- row_weight: float32 [2048], P('row'), may hold values from 0.3 to 3
- matches: int32 [2048], P('row'), may hold values from 0 to 16383
Outputs:
- grad_source: float32 [2048, 256], P(('row', 'col', 'depth'))
- grad_target: float32 [16384, 256], P(('col', 'depth', 'row'))
All inputs are finite; a program needn't handle non-finite values.
Results may differ from a plain program's by a relative error of at most 0.0029.
Values may be sent and summed in bfloat16 or wider, within the bound.
A program may use at most 64 MiB of HBM per device.

v0:
```python
import functools
import jax
import jax.numpy as jnp
from jax import lax
from jax.experimental import pallas as pl
from jax.experimental.pallas import tpu as pltpu
from jax.sharding import PartitionSpec as P

score_scale = 0.1875
F32 = jnp.float32
BF16 = jnp.bfloat16


def kernel(R, NC, ND, src_h, tgt_h, dual_h, weight_h, match_h, gs_out, gt_out,
           tgt, dual_all, weight, match_in, S, T2, dual, dual2, wm, wm_all, wm_g, dcol, e_buf, m_buf, lam,
           dbuf, ps, px, zs, zr, partf, gt_send, gt_recv,
           s_in, s_pair, r_pair, s_z, r_z, s_x, r_x, s_wm, r_wm, s_l, r_l, s_p, r_p, s_zp, r_zp, line_in):
    G = (NC // 2) * ND
    N = R * G
    n, D = src_h.shape
    own = tgt_h.shape[0]
    C = R * n
    row = lax.axis_index("row")
    col = lax.axis_index("col")
    dep = lax.axis_index("depth")
    par = lax.rem(col, 2)
    grp = (col // 2) * ND + dep
    me = grp * R + row
    sib_col = col + 1 - 2 * par
    order = sorted(range(G), key=lambda g: abs(2 * g - G + 1))
    MESH = pl.DeviceIdType.MESH

    def dev(r, c, d):
        return {"row": r, "col": c, "depth": d}

    sib = dev(row, sib_col, dep)

    def xpeer(k):
        return ring[k], dev(ring[k], col, dep)

    def zdev(g):
        return dev(row, (g // ND) * 2 + par, g % ND)

    def peer(k):
        i = lax.rem(me + k, N)
        g = i // R
        return dev(lax.rem(i, R), (g // ND) * 2 + par, lax.rem(g, ND))

    def rcopy(a, b, ss, rs, to):
        return pltpu.make_async_remote_copy(src_ref=a, dst_ref=b, send_sem=ss, recv_sem=rs,
                                            device_id=to, device_id_type=MESH)

    ring = [lax.rem(row + j, R) for j in range(R)]

    def each_peer(fn):
        if N <= 32:
            for g in range(G):
                for j in range(R - 1, 0, -1):
                    fn(dev(ring[j], (g // ND) * 2 + par, g % ND))

                @pl.when(grp != g)
                def _(g=g):
                    fn(zdev(g))
        else:
            lax.fori_loop(1, N, lambda k, c: (fn(peer(k)), c)[1], 0)

    barrier = pltpu.get_barrier_semaphore()
    pl.semaphore_signal(barrier, inc=1, device_id=sib, device_id_type=MESH)
    for j in range(1, R):
        pl.semaphore_signal(barrier, inc=1, device_id=xpeer(j)[1], device_id_type=MESH)
    for g in range(G):
        @pl.when(grp != g)
        def _(g=g):
            pl.semaphore_signal(barrier, inc=1, device_id=zdev(g), device_id_type=MESH)
    loads = [pltpu.make_async_copy(a, b, s_in.at[i]) for i, (a, b) in enumerate((
        (src_h, S.at[grp, row]), (tgt_h, tgt), (dual_h, dual_all), (weight_h, weight), (match_h, match_in)))]
    for c in loads:
        c.start()
    for c in loads[2:]:
        c.wait()

    dual[...] = dual_all[:, pl.ds(pl.multiple_of(row * own, own), own)]
    for i, vec in ((0, weight[...]), (1, match_in[...].astype(F32))):
        span = ND * n
        parts = [jnp.where(par == 0, vec[:, 2 * c * span:(2 * c + 1) * span],
                           vec[:, (2 * c + 1) * span:(2 * c + 2) * span]) for c in range(NC // 2)]
        wm[i:i + 1, :] = parts[0] if len(parts) == 1 else jnp.concatenate(parts, axis=1)
    wm_all[row] = wm[...]
    dcol[0:own, :] = jnp.transpose(jnp.broadcast_to(dual[...], (128, own)))
    for c in loads[:2]:
        c.wait()
    pl.semaphore_wait(barrier, R + G - 1)

    sends = []

    def go(c):
        c.start()
        sends.append(c)

    mine_s = S.at[grp, row]

    def z_send(g):
        return rcopy(mine_s, S.at[grp, row], s_z.at[g], r_z.at[grp], zdev(g))

    def x_send(g, j):
        return rcopy(S.at[g, row], S.at[g, row], s_x.at[j, g], r_x.at[row, g], xpeer(j)[1])

    for g in order:
        @pl.when(grp != g)
        def _(g=g):
            z_send(g).start()
    for j in range(1, R):
        x_send(grp, j).start()
    go(rcopy(tgt, T2, s_pair.at[0], r_pair.at[0], sib))
    go(rcopy(dual, dual2, s_pair.at[1], r_pair.at[1], sib))
    for g in order:
        @pl.when(grp != g)
        def _(g=g):
            rcopy(mine_s, S.at[g, row], s_z.at[g], r_z.at[g], zdev(g)).wait_recv()
            for j in range(1, R):
                x_send(g, j).start()
    for k in range(1, R):
        pl.semaphore_signal(line_in, inc=1, device_id=xpeer(k)[1], device_id_type=MESH)
        go(rcopy(wm, wm_all.at[row], s_wm.at[k], r_wm.at[row], xpeer(k)[1]))
    rcopy(dual, dual2, s_pair.at[1], r_pair.at[1], sib).wait_recv()
    dcol[own:2 * own, :] = jnp.transpose(jnp.broadcast_to(dual2[...], (128, own)))
    rcopy(tgt, T2, s_pair.at[0], r_pair.at[0], sib).wait_recv()

    lane_rep = C // 128

    def scores_chunk(g):
        rows = S[g].reshape(C, D)
        tops = []
        for h, t in ((0, tgt), (1, T2)):
            p = lax.dot_general(t[...], rows, (((1,), (1,)), ((), ())), preferred_element_type=F32)
            dc = dcol[h * own:(h + 1) * own, :]
            s = score_scale * p + jnp.concatenate([dc] * lane_rep, axis=1)
            e_buf[g, h * own:(h + 1) * own, :] = s
            tops.append(jnp.max(s, axis=0, keepdims=True))
        top = jnp.maximum(tops[0], tops[1])
        m_buf[g] = top
        e = jnp.exp(e_buf[g] - top)
        e_buf[g] = e
        lam[g, me] = top + jnp.log(jnp.sum(e, axis=0, keepdims=True))

    def gather_wait(g):
        for j in range(1, R):
            r, to = xpeer(j)
            rcopy(mine_s, S.at[g, r], s_x.at[0, 0], r_x.at[r, g], to).wait_recv()

    for i, g in enumerate(order):
        gather_wait(g)
        scores_chunk(g)
        if i == 0:
            pl.semaphore_wait(line_in, R - 1)
        each_peer(lambda to: rcopy(lam.at[g, me], lam.at[g, me], s_l.at[g], r_l.at[g], to).start())

    for k in range(1, R):
        r, to = xpeer(k)
        rcopy(wm, wm_all.at[r], s_wm.at[k], r_wm.at[r], to).wait_recv()
    for g in range(G):
        for i in range(2):
            wm_g[g, i:i + 1, :] = jnp.concatenate(
                [wm_all[r, i:i + 1, g * n:(g + 1) * n] for r in range(R)], axis=1)

    first = [((c * ND + dep) * R + row) * own for c in (col, sib_col)]

    def lam_all(g):
        every = lam.at[g, pl.ds(0, N - 1)]
        return rcopy(every, every, s_l.at[g], r_l.at[g], sib)

    def delta_chunk(g):
        lam_all(g).wait_recv()
        parts = lam[g]
        peak = jnp.max(parts, axis=0)
        log_total = peak + jnp.log(jnp.sum(jnp.exp(parts - peak[None]), axis=0))
        w = wm_g[g, 0:1, :]
        match = wm_g[g, 1:2, :].astype(jnp.int32)
        scale = w * jnp.exp(m_buf[g] - log_total)
        part = None
        for h, t in ((0, tgt), (1, T2)):
            ids = lax.broadcasted_iota(jnp.int32, (own, C), 0)
            hit = jnp.where(ids == match - first[h], w, 0.0)
            d = (scale * e_buf[g, h * own:(h + 1) * own, :] - hit).astype(BF16)
            dbuf[g, h * own:(h + 1) * own, :] = d
            q = lax.dot_general(d, t[...], (((0,), (0,)), ((), ())), preferred_element_type=F32)
            part = q if part is None else part + q
        return part

    for g in order:
        part = delta_chunk(g).reshape(R, n, D)
        partf[g] = part
        ps[g] = part.astype(BF16)
        for k in range(1, R):
            r, to = xpeer(k)
            go(rcopy(ps.at[g, r], px.at[g, row], s_p.at[k, g], r_p.at[row, g], to))

    def gt_half(h):
        acc = None
        for g in range(G):
            q = jnp.dot(dbuf[g, h * own:(h + 1) * own, :], S[g].reshape(C, D), preferred_element_type=F32)
            acc = q if acc is None else acc + q
        return acc

    gt_send[...] = gt_half(1)
    go(rcopy(gt_send, gt_recv, s_pair.at[2], r_pair.at[2], sib))

    def stage_sum(g):
        acc = partf[g, row]
        for k in range(1, R):
            acc = acc + px[g, ring[k]].astype(F32)
        return acc

    def zp_send(g):
        return rcopy(zs.at[g], zr.at[grp], s_zp.at[g], r_zp.at[grp], zdev(g))

    for g in order:
        for k in range(1, R):
            r, to = xpeer(k)
            rcopy(ps.at[g, r], px.at[g, r], s_p.at[k, 0], r_p.at[r, g], to).wait_recv()
        zs[g] = stage_sum(g).astype(BF16)

        @pl.when(grp != g)
        def _(g=g):
            zp_send(g).start()

    gt_out[...] = gt_half(0)
    rcopy(gt_send, gt_recv, s_pair.at[2], r_pair.at[2], sib).wait_recv()
    gt_out[...] = score_scale * (gt_out[...] + gt_recv[...])

    gs_out[...] = stage_sum(grp)
    for g in order:
        @pl.when(grp != g)
        def _(g=g):
            rcopy(zs.at[g], zr.at[g], s_zp.at[g], r_zp.at[g], zdev(g)).wait_recv()
            gs_out[...] = gs_out[...] + zr[g].astype(F32)
    gs_out[...] = score_scale * gs_out[...]

    for c in sends:
        c.wait_send()
    for g in range(G):
        lam_all(g).wait_send()
        for j in range(1, R):
            x_send(g, j).wait_send()

        @pl.when(grp != g)
        def _(g=g):
            z_send(g).wait_send()
            zp_send(g).wait_send()


def flush(gs, gt, gs_out, gt_out, sem):
    copies = [pltpu.make_async_copy(gt, gt_out, sem.at[0]), pltpu.make_async_copy(gs, gs_out, sem.at[1])]
    for c in copies:
        c.start()
    for c in copies:
        c.wait()


def per_device(R, NC, ND, source_desc, target_desc, target_dual, row_weight, matches):
    n, D = source_desc.shape
    own = target_desc.shape[0]
    G = (NC // 2) * ND
    C = R * n
    vm = pl.BlockSpec(memory_space=pltpu.VMEM)
    dma = pltpu.SemaphoreType.DMA
    outs = pl.pallas_call(
        functools.partial(kernel, R, NC, ND),
        out_shape=(jax.ShapeDtypeStruct((n, D), F32), jax.ShapeDtypeStruct((own, D), F32)),
        in_specs=[pl.BlockSpec(memory_space=pltpu.HBM)] * 5,
        out_specs=(vm, vm),
        scratch_shapes=[
            pltpu.VMEM((own, D), BF16),
            pltpu.VMEM((1, target_dual.shape[0]), F32),
            pltpu.VMEM((1, row_weight.shape[0]), F32),
            pltpu.VMEM((1, row_weight.shape[0]), jnp.int32),
            pltpu.VMEM((G, R, n, D), BF16),
            pltpu.VMEM((own, D), BF16),
            pltpu.VMEM((1, own), F32),
            pltpu.VMEM((1, own), F32),
            pltpu.VMEM((2, G * n), F32),
            pltpu.VMEM((R, 2, G * n), F32),
            pltpu.VMEM((G, 2, C), F32),
            pltpu.VMEM((2 * own, 128), F32),
            pltpu.VMEM((G, 2 * own, C), F32),
            pltpu.VMEM((G, 1, C), F32),
            pltpu.VMEM((G, R * G, 1, C), F32),
            pltpu.VMEM((G, 2 * own, C), BF16),
            pltpu.VMEM((G, R, n, D), BF16),
            pltpu.VMEM((G, R, n, D), BF16),
            pltpu.VMEM((G, n, D), BF16),
            pltpu.VMEM((G, n, D), BF16),
            pltpu.VMEM((G, R, n, D), F32),
            pltpu.VMEM((own, D), F32),
            pltpu.VMEM((own, D), F32),
            dma((5,)),
            dma((3,)), dma((3,)),
            dma((G,)), dma((G,)),
            dma((R, G)), dma((R, G)),
            dma((R,)), dma((R,)),
            dma((G,)), dma((G,)),
            dma((R, G)), dma((R, G)),
            dma((G,)), dma((G,)),
            pltpu.SemaphoreType.REGULAR,
        ],
        compiler_params=pltpu.CompilerParams(collective_id=0, has_side_effects=True,
                                             vmem_limit_bytes=32 * 1024 * 1024),
    )(*[pltpu.with_memory_space_constraint(a, pltpu.HBM) for a in (
        source_desc, target_desc, target_dual[None, :], row_weight[None, :], matches[None, :])])
    hbm = pl.BlockSpec(memory_space=pltpu.HBM)
    return pl.pallas_call(
        flush,
        out_shape=(jax.ShapeDtypeStruct((n, D), F32), jax.ShapeDtypeStruct((own, D), F32)),
        in_specs=[vm, vm],
        out_specs=(hbm, hbm),
        scratch_shapes=[dma((2,))],
        compiler_params=pltpu.CompilerParams(vmem_limit_bytes=8 * 1024 * 1024),
    )(*outs)


def solution(mesh):
    R, NC, ND = mesh.shape["row"], mesh.shape["col"], mesh.shape["depth"]
    return jax.shard_map(
        functools.partial(per_device, R, NC, ND),
        mesh=mesh,
        in_specs=(
            P(("row", "col", "depth"), None),
            P(("col", "depth", "row"), None),
            P(("col", "depth")),
            P("row"),
            P("row"),
        ),
        out_specs=(P(("row", "col", "depth"), None), P(("col", "depth", "row"), None)),
        check_vma=False,
    )
```

profile of v0, /device:TPU:0, one launch (start us, length us, event | category | flops | bytes accessed | tf_op | source)
XLA Modules:
  0.0 30.4 jit_solution(7028827164422749407)
XLA Ops:
  0.6 28.9 %shard_map.68 = (f32[64,256]{1,0:T(8,128)S(1)}, f32[512,256]{1,0:T(8,128)S(1)}) custom-call(bf16[64,256]{1,0:T(8,128)(2,1)} %src_h.1, bf16[512,256]{1,0:T(8,128)(2,1)} %tgt_h.1, f32[1,2048]{1,0:T(1,128)} %bitcast.3, f32[1,512]{1,0:T(1,128)} %bitcast.4, s32[1,512]{1,0:T(1,128)} %bitcast.5), custom_call_target="tpu_custom_call" | custom-call | tf_op jit(solution)/shard_map/pallas_call | solution.py:267
  29.6 0.8 %shard_map.69 = (f32[64,256]{1,0:T(8,128)}, f32[512,256]{1,0:T(8,128)}) custom-call(f32[64,256]{1,0:T(8,128)S(1)} %get-tuple-element.4.gs, f32[512,256]{1,0:T(8,128)S(1)} %get-tuple-element.5.gt), custom_call_target="tpu_custom_call" | custom-call | tf_op jit(solution)/shard_map/pallas_call | solution.py:311
where the time goes:
time: 30.5 us; the launch traced here: 30.4 us
  Pallas kernels  29.7 us (97%)
  between operations  0.64 us (2%)
    pallas_call x1, Pallas kernels, per_device(): pl.pallas_call(functools.partial(kernel, R, NC, ND), out_shape=(jax.Shape...  28.9 us
    pallas_call x1, Pallas kernels, per_device(): pl.pallas_call(flush, out_shape=(jax.ShapeDtypeStruct((n, D), F32), jax.S...  0.82 us

commit v1 on v0

v1 whole, which is shorter than its diff:
```python
import functools
import jax
import jax.numpy as jnp
from jax import lax
from jax.experimental import pallas as pl
from jax.experimental.pallas import tpu as pltpu
from jax.sharding import PartitionSpec as P

score_scale = 0.1875
F32 = jnp.float32
BF16 = jnp.bfloat16


def kernel(R, NC, ND, src_h, tgt_h, dual_h, weight_h, match_h, gs_out, gt_out,
           tgt, dual_all, weight, match_in, S, Q, QD, T2, dual, dual2, wm, wm_all, wm_g, dcol, e_buf, m_buf, lam,
           dbuf, ps, px, zs, zr, zd, ds, dr, partf, gt_send, gt_recv,
           s_in, s_pair, r_pair, s_z, r_z, s_x, r_x, s_qd, r_qd, s_d, s_wm, r_wm, s_l, r_l, s_p, r_p, s_zp, r_zp,
           s_zd, r_zd, s_dr, r_dr, line_in):
    G = (NC // 2) * ND
    N = R * G
    n, D = src_h.shape
    own = tgt_h.shape[0]
    C = R * n
    row = lax.axis_index("row")
    col = lax.axis_index("col")
    dep = lax.axis_index("depth")
    par = lax.rem(col, 2)
    grp = (col // 2) * ND + dep
    me = grp * R + row
    sib_col = col + 1 - 2 * par
    order = sorted(range(G), key=lambda g: abs(2 * g - G + 1))
    MESH = pl.DeviceIdType.MESH

    def flip(j):
        r, b = row, 1
        while b < R:
            if j & b:
                r = r + b * (1 - 2 * lax.rem(row // b, 2))
            b *= 2
        return r

    if R & (R - 1) == 0:
        rows = [flip(j) for j in range(R)]
    else:
        rows = [lax.rem(row + j, R) for j in range(R)]
    far = R >= 4 and R & (R - 1) == 0
    near = range(1, R - 1) if far else range(1, R)
    rd = rows[R - 1]

    def dev(r, c, d):
        return {"row": r, "col": c, "depth": d}

    sib = dev(row, sib_col, dep)

    def zdev(g):
        return dev(row, (g // ND) * 2 + par, g % ND)

    def zrel(g):
        return dev(row, (g // ND) * 2 + 1 - par, g % ND)

    def xdev(j):
        return dev(rows[j], col, dep)

    def xrel(j):
        return dev(rows[j], sib_col, dep)

    def peer(k):
        i = lax.rem(me + k, N)
        g = i // R
        return dev(lax.rem(i, R), (g // ND) * 2 + par, lax.rem(g, ND))

    def rcopy(a, b, ss, rs, to):
        return pltpu.make_async_remote_copy(src_ref=a, dst_ref=b, send_sem=ss, recv_sem=rs,
                                            device_id=to, device_id_type=MESH)

    def each_peer(fn):
        if N <= 32:
            for g in range(G):
                for j in range(R - 1, 0, -1):
                    fn(dev(rows[j], (g // ND) * 2 + par, g % ND))

                @pl.when(grp != g)
                def _(g=g):
                    fn(zdev(g))
        else:
            lax.fori_loop(1, N, lambda k, c: (fn(peer(k)), c)[1], 0)

    def greet(sem, to):
        pl.semaphore_signal(sem, inc=1, device_id=to, device_id_type=MESH)

    barrier = pltpu.get_barrier_semaphore()
    for g in range(G):
        @pl.when(grp != g)
        def _(g=g):
            greet(barrier, zrel(g))
    for j in near:
        greet(barrier, xdev(j))
        greet(barrier, xrel(j))
    if far:
        greet(barrier, xrel(R - 1))
    greet(barrier, sib)
    loads = [pltpu.make_async_copy(a, b, s_in.at[i]) for i, (a, b) in enumerate((
        (src_h, S.at[grp, row]), (tgt_h, tgt), (dual_h, dual_all), (weight_h, weight), (match_h, match_in)))]
    for c in loads:
        c.start()
    pl.semaphore_wait(barrier, G + 2 * len(near) + (1 if far else 0))

    sends = []

    def go(c):
        c.start()
        sends.append(c)

    mine = src_h

    def z_send(g):
        return rcopy(mine, Q.at[grp], s_z.at[g], r_z.at[grp], zrel(g))

    for g in order:
        @pl.when(grp != g)
        def _(g=g):
            z_send(g).start()
    if far:
        go(rcopy(mine, QD, s_qd, r_qd, xrel(R - 1)))
    for j in near:
        rcopy(mine, S.at[grp, row], s_x.at[j, grp], r_x.at[row, grp], xdev(j)).start()
    go(rcopy(tgt_h, T2, s_pair.at[0], r_pair.at[0], sib))
    for j in range(1, R):
        greet(line_in, xrel(j))
    greet(line_in, sib)
    for c in loads[2:]:
        c.wait()
    dual[...] = dual_all[:, pl.ds(pl.multiple_of(row * own, own), own)]
    go(rcopy(dual, dual2, s_pair.at[1], r_pair.at[1], sib))

    for i, vec in ((0, weight[...]), (1, match_in[...].astype(F32))):
        span = ND * n
        for q in range(2):
            parts = [jnp.where(par == q, vec[:, 2 * c * span:(2 * c + 1) * span],
                               vec[:, (2 * c + 1) * span:(2 * c + 2) * span]) for c in range(NC // 2)]
            wm[q, i:i + 1, :] = parts[0] if len(parts) == 1 else jnp.concatenate(parts, axis=1)
    wm_all[row] = wm[0]
    for j in range(1, R):
        go(rcopy(wm.at[1], wm_all.at[row], s_wm.at[j], r_wm.at[row], xrel(j)))

    def x_send(g, j):
        return rcopy(Q.at[g], S.at[g, row], s_x.at[j, g], r_x.at[row, g], sib if j == 0 else xrel(j))

    def d_send(g):
        return rcopy(QD, S.at[grp, rd], s_d.at[g], r_x.at[rd, grp], zrel(g))

    hops = [0] + list(near)
    if far:
        rcopy(QD, QD, s_qd, r_qd, xrel(R - 1)).wait_recv()
        for g in order:
            d_send(g).start()
    for g in order:
        @pl.when(grp != g)
        def _(g=g):
            rcopy(Q.at[g], Q.at[g], s_z.at[g], r_z.at[g], zrel(g)).wait_recv()
            for j in list(near) + [0]:
                x_send(g, j).start()
    dcol[0:own, :] = jnp.transpose(jnp.broadcast_to(dual[...], (128, own)))
    for c in loads[:2]:
        c.wait()
    rcopy(dual, dual2, s_pair.at[1], r_pair.at[1], sib).wait_recv()
    dcol[own:2 * own, :] = jnp.transpose(jnp.broadcast_to(dual2[...], (128, own)))
    rcopy(tgt, T2, s_pair.at[0], r_pair.at[0], sib).wait_recv()

    lane_rep = C // 128

    def scores_chunk(g):
        block = S[g].reshape(C, D)
        tops = []
        for h, t in ((0, tgt), (1, T2)):
            p = lax.dot_general(t[...], block, (((1,), (1,)), ((), ())), preferred_element_type=F32)
            dc = dcol[h * own:(h + 1) * own, :]
            s = score_scale * p + jnp.concatenate([dc] * lane_rep, axis=1)
            e_buf[g, h * own:(h + 1) * own, :] = s
            tops.append(jnp.max(s, axis=0, keepdims=True))
        top = jnp.maximum(tops[0], tops[1])
        m_buf[g] = top
        e = jnp.exp(e_buf[g] - top)
        e_buf[g] = e
        lam[g, me] = top + jnp.log(jnp.sum(e, axis=0, keepdims=True))

    def take(g, r):
        rcopy(S.at[g, r], S.at[g, r], s_x.at[0, 0], r_x.at[r, g], sib).wait_recv()

    place = sum(i * (grp == g).astype(jnp.int32) for i, g in enumerate(order))
    for i in range(G):
        g = grp if i == 0 else jnp.where(place >= i, order[i - 1], order[i])
        for j in range(0 if i else 1, R):
            take(g, rows[j])
        scores_chunk(g)
        if i == 0:
            pl.semaphore_wait(line_in, R)
        each_peer(lambda to: rcopy(lam.at[g, me], lam.at[g, me], s_l.at[g], r_l.at[g], to).start())

    for j in range(1, R):
        rcopy(wm.at[1], wm_all.at[rows[j]], s_wm.at[j], r_wm.at[rows[j]], xrel(j)).wait_recv()
    for g in range(G):
        for i in range(2):
            wm_g[g, i:i + 1, :] = jnp.concatenate(
                [wm_all[r, i:i + 1, g * n:(g + 1) * n] for r in range(R)], axis=1)

    first = [((c * ND + dep) * R + row) * own for c in (col, sib_col)]

    def lam_all(g):
        every = lam.at[g, pl.ds(0, N - 1)]
        return rcopy(every, every, s_l.at[g], r_l.at[g], sib)

    def delta_chunk(g):
        lam_all(g).wait_recv()
        parts = lam[g]
        peak = jnp.max(parts, axis=0)
        log_total = peak + jnp.log(jnp.sum(jnp.exp(parts - peak[None]), axis=0))
        w = wm_g[g, 0:1, :]
        match = wm_g[g, 1:2, :].astype(jnp.int32)
        scale = w * jnp.exp(m_buf[g] - log_total)
        part = None
        for h, t in ((0, tgt), (1, T2)):
            ids = lax.broadcasted_iota(jnp.int32, (own, C), 0)
            hit = jnp.where(ids == match - first[h], w, 0.0)
            d = (scale * e_buf[g, h * own:(h + 1) * own, :] - hit).astype(BF16)
            dbuf[g, h * own:(h + 1) * own, :] = d
            q = lax.dot_general(d, t[...], (((0,), (0,)), ((), ())), preferred_element_type=F32)
            part = q if part is None else part + q
        return part

    def p_send(g, j):
        apart = (grp != g).astype(jnp.int32)
        to = sib if j == 0 else dev(rows[j], col + apart * (sib_col - col), dep)
        return rcopy(ps.at[g, rows[j]], px.at[g, row], s_p.at[j, g], r_p.at[row, g], to)

    def far_send(g):
        return rcopy(ps.at[g, rd], zd.at[grp], s_zd.at[g], r_zd.at[grp], zrel(g))

    def gt_half(h, groups):
        acc = None
        for g in groups:
            q = jnp.dot(dbuf[g, h * own:(h + 1) * own, :], S[g].reshape(C, D), preferred_element_type=F32)
            acc = q if acc is None else acc + q
        return acc

    for i, g in enumerate(order):
        if i == G - 1 and G > 1:
            gt_send[...] = gt_half(1, order[:-1])
            gt_out[...] = gt_half(0, order[:-1])
        part = delta_chunk(g).reshape(R, n, D)
        ps[g] = part.astype(BF16)
        if far:
            far_send(g).start()
        for j in near:
            p_send(g, j).start()

        @pl.when(grp != g)
        def _(g=g):
            p_send(g, 0).start()

        @pl.when(grp == g)
        def _(part=part):
            partf[...] = part

    last = order[-1:]
    gt_send[...] = gt_send[...] + gt_half(1, last) if G > 1 else gt_half(1, last)
    go(rcopy(gt_send, gt_recv, s_pair.at[2], r_pair.at[2], sib))

    def taken(g, j):
        rcopy(ps.at[g, rows[j]], px.at[g, rows[j]], s_p.at[j, g], r_p.at[rows[j], g], sib).wait_recv()
        return px[g, rows[j]].astype(F32)

    def zp_send(g):
        return rcopy(zs.at[g], zr.at[grp], s_zp.at[g], r_zp.at[grp], zrel(g))

    def relay(g):
        @pl.when(grp != g)
        def _():
            acc = taken(g, 0)
            for j in near:
                acc = acc + taken(g, j)
            zs[g] = acc.astype(BF16)
            zp_send(g).start()

    def far_copy():
        return rcopy(ds, dr, s_dr, r_dr, xrel(R - 1))

    def far_relay():
        acc = None
        for g in range(G):
            rcopy(zs.at[g], zd.at[g], s_zd.at[g], r_zd.at[g], sib).wait_recv()
            acc = zd[g].astype(F32) if acc is None else acc + zd[g].astype(F32)
        ds[...] = acc.astype(BF16)
        far_copy().start()

    for g in order[:-1]:
        relay(g)
    if far:
        pl.when(grp != order[-1])(far_relay)
    relay(order[-1])
    if far:
        pl.when(grp == order[-1])(far_relay)

    gt_mine = gt_out[...] + gt_half(0, last) if G > 1 else gt_half(0, last)
    rcopy(gt_send, gt_recv, s_pair.at[2], r_pair.at[2], sib).wait_recv()
    gt_out[...] = score_scale * (gt_mine + gt_recv[...])

    acc = partf[row]
    for j in near:
        acc = acc + taken(grp, j)
    gs_out[...] = acc
    for g in order:
        @pl.when(grp != g)
        def _(g=g):
            rcopy(zs.at[g], zr.at[g], s_zp.at[g], r_zp.at[g], sib).wait_recv()
            gs_out[...] = gs_out[...] + zr[g].astype(F32)
    if far:
        far_copy().wait_recv()
        gs_out[...] = score_scale * (gs_out[...] + dr[...].astype(F32))
    else:
        gs_out[...] = score_scale * gs_out[...]

    for c in sends:
        c.wait_send()
    if far:
        far_copy().wait_send()
    for g in range(G):
        lam_all(g).wait_send()
        for j in near:
            x_send(g, j).wait_send()
            p_send(g, j).wait_send()
        if far:
            d_send(g).wait_send()
            far_send(g).wait_send()

        @pl.when(grp != g)
        def _(g=g):
            z_send(g).wait_send()
            x_send(g, 0).wait_send()
            p_send(g, 0).wait_send()
            zp_send(g).wait_send()


def flush(gs, gt, gs_out, gt_out, sem):
    copies = [pltpu.make_async_copy(gt, gt_out, sem.at[0]), pltpu.make_async_copy(gs, gs_out, sem.at[1])]
    for c in copies:
        c.start()
    for c in copies:
        c.wait()


def per_device(R, NC, ND, source_desc, target_desc, target_dual, row_weight, matches):
    n, D = source_desc.shape
    own = target_desc.shape[0]
    G = (NC // 2) * ND
    C = R * n
    vm = pl.BlockSpec(memory_space=pltpu.VMEM)
    dma = pltpu.SemaphoreType.DMA
    outs = pl.pallas_call(
        functools.partial(kernel, R, NC, ND),
        out_shape=(jax.ShapeDtypeStruct((n, D), F32), jax.ShapeDtypeStruct((own, D), F32)),
        in_specs=[pl.BlockSpec(memory_space=pltpu.HBM)] * 5,
        out_specs=(vm, vm),
        scratch_shapes=[
            pltpu.VMEM((own, D), BF16),
            pltpu.VMEM((1, target_dual.shape[0]), F32),
            pltpu.VMEM((1, row_weight.shape[0]), F32),
            pltpu.VMEM((1, row_weight.shape[0]), jnp.int32),
            pltpu.VMEM((G, R, n, D), BF16),
            pltpu.VMEM((G, n, D), BF16),
            pltpu.VMEM((n, D), BF16),
            pltpu.VMEM((own, D), BF16),
            pltpu.VMEM((1, own), F32),
            pltpu.VMEM((1, own), F32),
            pltpu.VMEM((2, 2, G * n), F32),
            pltpu.VMEM((R, 2, G * n), F32),
            pltpu.VMEM((G, 2, C), F32),
            pltpu.VMEM((2 * own, 128), F32),
            pltpu.VMEM((G, 2 * own, C), F32),
            pltpu.VMEM((G, 1, C), F32),
            pltpu.VMEM((G, R * G, 1, C), F32),
            pltpu.VMEM((G, 2 * own, C), BF16),
            pltpu.VMEM((G, R, n, D), BF16),
            pltpu.VMEM((G, R, n, D), BF16),
            pltpu.VMEM((G, n, D), BF16),
            pltpu.VMEM((G, n, D), BF16),
            pltpu.VMEM((G, n, D), BF16),
            pltpu.VMEM((n, D), BF16),
            pltpu.VMEM((n, D), BF16),
            pltpu.VMEM((R, n, D), F32),
            pltpu.VMEM((own, D), F32),
            pltpu.VMEM((own, D), F32),
            dma((5,)),
            dma((3,)), dma((3,)),
            dma((G,)), dma((G,)),
            dma((R, G)), dma((R, G)),
            dma, dma,
            dma((G,)),
            dma((R,)), dma((R,)),
            dma((G,)), dma((G,)),
            dma((R, G)), dma((R, G)),
            dma((G,)), dma((G,)),
            dma((G,)), dma((G,)),
            dma, dma,
            pltpu.SemaphoreType.REGULAR,
        ],
        compiler_params=pltpu.CompilerParams(collective_id=0, has_side_effects=True,
                                             vmem_limit_bytes=32 * 1024 * 1024),
    )(*[pltpu.with_memory_space_constraint(a, pltpu.HBM) for a in (
        source_desc, target_desc, target_dual[None, :], row_weight[None, :], matches[None, :])])
    hbm = pl.BlockSpec(memory_space=pltpu.HBM)
    return pl.pallas_call(
        flush,
        out_shape=(jax.ShapeDtypeStruct((n, D), F32), jax.ShapeDtypeStruct((own, D), F32)),
        in_specs=[vm, vm],
        out_specs=(hbm, hbm),
        scratch_shapes=[dma((2,))],
        compiler_params=pltpu.CompilerParams(vmem_limit_bytes=8 * 1024 * 1024),
    )(*outs)


def solution(mesh):
    R, NC, ND = mesh.shape["row"], mesh.shape["col"], mesh.shape["depth"]
    return jax.shard_map(
        functools.partial(per_device, R, NC, ND),
        mesh=mesh,
        in_specs=(
            P(("row", "col", "depth"), None),
            P(("col", "depth", "row"), None),
            P(("col", "depth")),
            P("row"),
            P("row"),
        ),
        out_specs=(P(("row", "col", "depth"), None), P(("col", "depth", "row"), None)),
        check_vma=False,
    )
```

time: 30.5 us -> 29.5 us (0.967)
  Pallas kernels: 29.7 us -> 28.7 us
    pallas_call x1, Pallas kernels: 28.9 us -> 27.9 us  [per_device(): pl.pallas_call(functools.partial(kernel, R, NC, ND), out_shape=(jax.Shape...]
where the time goes in v1:
time: 29.5 us; the launch traced here: 29.3 us
  Pallas kernels  28.7 us (97%)
  between operations  0.64 us (2%)
    pallas_call x1, Pallas kernels, per_device(): pl.pallas_call(functools.partial(kernel, R, NC, ND), out_shape=(jax.Shape...  27.9 us
    pallas_call x1, Pallas kernels, per_device(): pl.pallas_call(flush, out_shape=(jax.ShapeDtypeStruct((n, D), F32), jax.S...  0.82 us

profile of v1, /device:TPU:0, one launch (start us, length us, event | category | flops | bytes accessed | tf_op | source)
XLA Modules:
  0.0 29.3 jit_solution(6877432261999675741)
XLA Ops:
  0.6 27.9 %shard_map.68 = (f32[64,256]{1,0:T(8,128)S(1)}, f32[512,256]{1,0:T(8,128)S(1)}) custom-call(bf16[64,256]{1,0:T(8,128)(2,1)} %src_h.1, bf16[512,256]{1,0:T(8,128)(2,1)} %tgt_h.1, f32[1,2048]{1,0:T(1,128)} %bitcast.3, f32[1,512]{1,0:T(1,128)} %bitcast.4, s32[1,512]{1,0:T(1,128)} %bitcast.5), custom_call_target="tpu_custom_call" | custom-call | tf_op jit(solution)/shard_map/pallas_call | solution.py:359
  28.5 0.8 %shard_map.69 = (f32[64,256]{1,0:T(8,128)}, f32[512,256]{1,0:T(8,128)}) custom-call(f32[64,256]{1,0:T(8,128)S(1)} %get-tuple-element.4.gs, f32[512,256]{1,0:T(8,128)S(1)} %get-tuple-element.5.gt), custom_call_target="tpu_custom_call" | custom-call | tf_op jit(solution)/shard_map/pallas_call | solution.py:412

commit v2 on v1

--- a/solution.py
+++ b/solution.py
@@ -28,7 +28,7 @@
     grp = (col // 2) * ND + dep
     me = grp * R + row
     sib_col = col + 1 - 2 * par
-    order = sorted(range(G), key=lambda g: abs(2 * g - G + 1))
+    order = list(range(G))
     MESH = pl.DeviceIdType.MESH
 
     def flip(j):
@@ -116,7 +116,8 @@
     def z_send(g):
         return rcopy(mine, Q.at[grp], s_z.at[g], r_z.at[grp], zrel(g))
 
-    for g in order:
+    tour = [jnp.where(grp == 0, G - 1 - k, k) for k in range(G)]
+    for g in tour:
         @pl.when(grp != g)
         def _(g=g):
             z_send(g).start()
@@ -152,7 +153,7 @@
     hops = [0] + list(near)
     if far:
         rcopy(QD, QD, s_qd, r_qd, xrel(R - 1)).wait_recv()
-        for g in order:
+        for g in tour:
             d_send(g).start()
     for g in order:
         @pl.when(grp != g)

time: 29.5 us -> 28.5 us (0.966)
  Pallas kernels: 28.7 us -> 27.7 us
    pallas_call x1, Pallas kernels: 27.9 us -> 26.9 us  [per_device(): pl.pallas_call(functools.partial(kernel, R, NC, ND), out_shape=(jax.Shape...]
where the time goes in v2:
time: 28.5 us; the launch traced here: 28.4 us
  Pallas kernels  27.7 us (97%)
  between operations  0.64 us (2%)
    pallas_call x1, Pallas kernels, per_device(): pl.pallas_call(functools.partial(kernel, R, NC, ND), out_shape=(jax.Shape...  26.9 us
    pallas_call x1, Pallas kernels, per_device(): pl.pallas_call(flush, out_shape=(jax.ShapeDtypeStruct((n, D), F32), jax.S...  0.82 us

profile of v2, /device:TPU:0, one launch (start us, length us, event | category | flops | bytes accessed | tf_op | source)
XLA Modules:
  0.0 28.4 jit_solution(2969815472021573839)
XLA Ops:
  0.6 26.9 %shard_map.68 = (f32[64,256]{1,0:T(8,128)S(1)}, f32[512,256]{1,0:T(8,128)S(1)}) custom-call(bf16[64,256]{1,0:T(8,128)(2,1)} %src_h.1, bf16[512,256]{1,0:T(8,128)(2,1)} %tgt_h.1, f32[1,2048]{1,0:T(1,128)} %bitcast.3, f32[1,512]{1,0:T(1,128)} %bitcast.4, s32[1,512]{1,0:T(1,128)} %bitcast.5), custom_call_target="tpu_custom_call" | custom-call | tf_op jit(solution)/shard_map/pallas_call | solution.py:360
  27.5 0.8 %shard_map.69 = (f32[64,256]{1,0:T(8,128)}, f32[512,256]{1,0:T(8,128)}) custom-call(f32[64,256]{1,0:T(8,128)S(1)} %get-tuple-element.4.gs, f32[512,256]{1,0:T(8,128)S(1)} %get-tuple-element.5.gt), custom_call_target="tpu_custom_call" | custom-call | tf_op jit(solution)/shard_map/pallas_call | solution.py:413

commit v3 on v2

--- a/solution.py
+++ b/solution.py
@@ -13,7 +13,7 @@
 
 def kernel(R, NC, ND, src_h, tgt_h, dual_h, weight_h, match_h, gs_out, gt_out,
            tgt, dual_all, weight, match_in, S, Q, QD, T2, dual, dual2, wm, wm_all, wm_g, dcol, e_buf, m_buf, lam,
-           dbuf, ps, px, zs, zr, zd, ds, dr, partf, gt_send, gt_recv,
+           dbuf, U, H, em, ps, px, zs, zr, zd, ds, dr, partf, gt_send, gt_recv,
            s_in, s_pair, r_pair, s_z, r_z, s_x, r_x, s_qd, r_qd, s_d, s_wm, r_wm, s_l, r_l, s_p, r_p, s_zp, r_zp,
            s_zd, r_zd, s_dr, r_dr, line_in):
     G = (NC // 2) * ND
@@ -103,6 +103,8 @@
         (src_h, S.at[grp, row]), (tgt_h, tgt), (dual_h, dual_all), (weight_h, weight), (match_h, match_in)))]
     for c in loads:
         c.start()
+    for c in loads[:2]:
+        c.wait()
     pl.semaphore_wait(barrier, G + 2 * len(near) + (1 if far else 0))
 
     sends = []
@@ -111,7 +113,7 @@
         c.start()
         sends.append(c)
 
-    mine = src_h
+    mine = S.at[grp, row]
 
     def z_send(g):
         return rcopy(mine, Q.at[grp], s_z.at[g], r_z.at[grp], zrel(g))
@@ -125,7 +127,7 @@
         go(rcopy(mine, QD, s_qd, r_qd, xrel(R - 1)))
     for j in near:
         rcopy(mine, S.at[grp, row], s_x.at[j, grp], r_x.at[row, grp], xdev(j)).start()
-    go(rcopy(tgt_h, T2, s_pair.at[0], r_pair.at[0], sib))
+    go(rcopy(tgt, T2, s_pair.at[0], r_pair.at[0], sib))
     for j in range(1, R):
         greet(line_in, xrel(j))
     greet(line_in, sib)
@@ -162,8 +164,6 @@
             for j in list(near) + [0]:
                 x_send(g, j).start()
     dcol[0:own, :] = jnp.transpose(jnp.broadcast_to(dual[...], (128, own)))
-    for c in loads[:2]:
-        c.wait()
     rcopy(dual, dual2, s_pair.at[1], r_pair.at[1], sib).wait_recv()
     dcol[own:2 * own, :] = jnp.transpose(jnp.broadcast_to(dual2[...], (128, own)))
     rcopy(tgt, T2, s_pair.at[0], r_pair.at[0], sib).wait_recv()
@@ -211,23 +211,56 @@
         every = lam.at[g, pl.ds(0, N - 1)]
         return rcopy(every, every, s_l.at[g], r_l.at[g], sib)
 
-    def delta_chunk(g):
+    halves = ((0, tgt), (1, T2))
+    over_targets = (((0,), (0,)), ((), ()))
+
+    def hits(g, h):
+        match = wm_g[g, 1:2, :].astype(jnp.int32)
+        return lax.broadcasted_iota(jnp.int32, (own, C), 0) == match - first[h]
+
+    def scale_of(g):
         lam_all(g).wait_recv()
         parts = lam[g]
         peak = jnp.max(parts, axis=0)
         log_total = peak + jnp.log(jnp.sum(jnp.exp(parts - peak[None]), axis=0))
-        w = wm_g[g, 0:1, :]
-        match = wm_g[g, 1:2, :].astype(jnp.int32)
-        scale = w * jnp.exp(m_buf[g] - log_total)
+        return wm_g[g, 0:1, :] * jnp.exp(m_buf[g] - log_total)
+
+    def round_delta(g, h, scale):
+        hit = jnp.where(hits(g, h), wm_g[g, 0:1, :], 0.0)
+        d = (scale * e_buf[g, h * own:(h + 1) * own, :] - hit).astype(BF16)
+        dbuf[g, h * own:(h + 1) * own, :] = d
+        return d
+
+    def delta_chunk(g):
+        scale = scale_of(g)
         part = None
-        for h, t in ((0, tgt), (1, T2)):
-            ids = lax.broadcasted_iota(jnp.int32, (own, C), 0)
-            hit = jnp.where(ids == match - first[h], w, 0.0)
-            d = (scale * e_buf[g, h * own:(h + 1) * own, :] - hit).astype(BF16)
-            dbuf[g, h * own:(h + 1) * own, :] = d
-            q = lax.dot_general(d, t[...], (((0,), (0,)), ((), ())), preferred_element_type=F32)
+        for h, t in halves:
+            q = lax.dot_general(round_delta(g, h, scale), t[...], over_targets, preferred_element_type=F32)
             part = q if part is None else part + q
         return part
+
+    def prepare(g):
+        u = k = m = None
+        for h, t in halves:
+            e = e_buf[g, h * own:(h + 1) * own, :]
+            hit = hits(g, h)
+            at = jnp.sum(jnp.where(hit, e, 0.0), axis=0, keepdims=True)
+            uh = lax.dot_general(jnp.where(hit, 0.0, e).astype(BF16), t[...], over_targets, preferred_element_type=F32)
+            kh = lax.dot_general(jnp.where(hit, 1.0, 0.0).astype(BF16), t[...], over_targets, preferred_element_type=F32)
+            u, k, m = (uh, kh, at) if h == 0 else (u + uh, k + kh, m + at)
+        U[...] = u
+        H[...] = k
+        em[...] = m
+
+    def prepared(g):
+        scale = scale_of(g)
+        m_buf[g] = scale
+        coef = (scale * em[...] - wm_g[g, 0:1, :]).astype(BF16).astype(F32)
+
+        def down(v):
+            return jnp.concatenate([jnp.transpose(jnp.broadcast_to(v, (128, C)))] * (D // 128), axis=1)
+
+        return down(scale) * U[...] + down(coef) * H[...]
 
     def p_send(g, j):
         apart = (grp != g).astype(jnp.int32)
@@ -244,28 +277,7 @@
             acc = q if acc is None else acc + q
         return acc
 
-    for i, g in enumerate(order):
-        if i == G - 1 and G > 1:
-            gt_send[...] = gt_half(1, order[:-1])
-            gt_out[...] = gt_half(0, order[:-1])
-        part = delta_chunk(g).reshape(R, n, D)
-        ps[g] = part.astype(BF16)
-        if far:
-            far_send(g).start()
-        for j in near:
-            p_send(g, j).start()
-
-        @pl.when(grp != g)
-        def _(g=g):
-            p_send(g, 0).start()
-
-        @pl.when(grp == g)
-        def _(part=part):
-            partf[...] = part
-
-    last = order[-1:]
-    gt_send[...] = gt_send[...] + gt_half(1, last) if G > 1 else gt_half(1, last)
-    go(rcopy(gt_send, gt_recv, s_pair.at[2], r_pair.at[2], sib))
+    prepare(order[0])
 
     def taken(g, j):
         rcopy(ps.at[g, rows[j]], px.at[g, rows[j]], s_p.at[j, g], r_p.at[rows[j], g], sib).wait_recv()
@@ -282,6 +294,32 @@
                 acc = acc + taken(g, j)
             zs[g] = acc.astype(BF16)
             zp_send(g).start()
+
+    for i, g in enumerate(order):
+        if i == G - 1 and G > 1:
+            gt_send[...] = gt_half(1, order[:-1])
+        part = (prepared(g) if i == 0 else delta_chunk(g)).reshape(R, n, D)
+        ps[g] = part.astype(BF16)
+        if far:
+            far_send(g).start()
+        for j in near:
+            p_send(g, j).start()
+
+        @pl.when(grp != g)
+        def _(g=g):
+            p_send(g, 0).start()
+
+        @pl.when(grp == g)
+        def _(part=part):
+            partf[...] = part
+
+        if i == 0:
+            for h in range(2):
+                round_delta(g, h, m_buf[g])
+
+    last = order[-1:]
+    gt_send[...] = gt_send[...] + gt_half(1, last) if G > 1 else gt_half(1, last)
+    go(rcopy(gt_send, gt_recv, s_pair.at[2], r_pair.at[2], sib))
 
     def far_copy():
         return rcopy(ds, dr, s_dr, r_dr, xrel(R - 1))
@@ -294,15 +332,12 @@
         ds[...] = acc.astype(BF16)
         far_copy().start()
 
-    for g in order[:-1]:
+    for i, g in enumerate(order):
         relay(g)
-    if far:
-        pl.when(grp != order[-1])(far_relay)
-    relay(order[-1])
-    if far:
-        pl.when(grp == order[-1])(far_relay)
-
-    gt_mine = gt_out[...] + gt_half(0, last) if G > 1 else gt_half(0, last)
+        if far:
+            pl.when(grp == g)(far_relay)
+
+    gt_mine = gt_half(0, order)
     rcopy(gt_send, gt_recv, s_pair.at[2], r_pair.at[2], sib).wait_recv()
     gt_out[...] = score_scale * (gt_mine + gt_recv[...])
 
@@ -381,6 +416,9 @@
             pltpu.VMEM((G, 1, C), F32),
             pltpu.VMEM((G, R * G, 1, C), F32),
             pltpu.VMEM((G, 2 * own, C), BF16),
+            pltpu.VMEM((C, D), F32),
+            pltpu.VMEM((C, D), F32),
+            pltpu.VMEM((1, C), F32),
             pltpu.VMEM((G, R, n, D), BF16),
             pltpu.VMEM((G, R, n, D), BF16),
             pltpu.VMEM((G, n, D), BF16),

time: 28.5 us -> 27.4 us (0.961)
  Pallas kernels: 27.7 us -> 26.3 us
    pallas_call x1, Pallas kernels: 26.9 us -> 25.5 us  [per_device(): pl.pallas_call(functools.partial(kernel, R, NC, ND), out_shape=(jax.Shape...]
where the time goes in v3:
time: 27.4 us; the launch traced here: 27 us
  Pallas kernels  26.3 us (96%)
  between operations  0.64 us (2%)
    pallas_call x1, Pallas kernels, per_device(): pl.pallas_call(functools.partial(kernel, R, NC, ND), out_shape=(jax.Shape...  25.5 us
    pallas_call x1, Pallas kernels, per_device(): pl.pallas_call(flush, out_shape=(jax.ShapeDtypeStruct((n, D), F32), jax.S...  0.82 us

profile of v3, /device:TPU:0, one launch (start us, length us, event | category | flops | bytes accessed | tf_op | source)
XLA Modules:
  0.0 27.0 jit_solution(14113141752105640571)
XLA Ops:
  0.6 25.5 %shard_map.68 = (f32[64,256]{1,0:T(8,128)S(1)}, f32[512,256]{1,0:T(8,128)S(1)}) custom-call(bf16[64,256]{1,0:T(8,128)(2,1)} %src_h.1, bf16[512,256]{1,0:T(8,128)(2,1)} %tgt_h.1, f32[1,2048]{1,0:T(1,128)} %bitcast.3, f32[1,512]{1,0:T(1,128)} %bitcast.4, s32[1,512]{1,0:T(1,128)} %bitcast.5), custom_call_target="tpu_custom_call" | custom-call | tf_op jit(solution)/shard_map/pallas_call | solution.py:395
  26.2 0.8 %shard_map.69 = (f32[64,256]{1,0:T(8,128)}, f32[512,256]{1,0:T(8,128)}) custom-call(f32[64,256]{1,0:T(8,128)S(1)} %get-tuple-element.4.gs, f32[512,256]{1,0:T(8,128)S(1)} %get-tuple-element.5.gt), custom_call_target="tpu_custom_call" | custom-call | tf_op jit(solution)/shard_map/pallas_call | solution.py:451

commit v4 on v3

--- a/solution.py
+++ b/solution.py
@@ -7,6 +7,7 @@
 from jax.sharding import PartitionSpec as P
 
 score_scale = 0.1875
+log2e = 1.4426950408889634
 F32 = jnp.float32
 BF16 = jnp.bfloat16
 
@@ -28,7 +29,7 @@
     grp = (col // 2) * ND + dep
     me = grp * R + row
     sib_col = col + 1 - 2 * par
-    order = list(range(G))
+    order = sorted(range(G), key=lambda g: (g > 0) - (g == G - 1))
     MESH = pl.DeviceIdType.MESH
 
     def flip(j):
@@ -163,9 +164,9 @@
             rcopy(Q.at[g], Q.at[g], s_z.at[g], r_z.at[g], zrel(g)).wait_recv()
             for j in list(near) + [0]:
                 x_send(g, j).start()
-    dcol[0:own, :] = jnp.transpose(jnp.broadcast_to(dual[...], (128, own)))
+    dcol[0:own, :] = jnp.transpose(jnp.broadcast_to(dual[...] * log2e, (128, own)))
     rcopy(dual, dual2, s_pair.at[1], r_pair.at[1], sib).wait_recv()
-    dcol[own:2 * own, :] = jnp.transpose(jnp.broadcast_to(dual2[...], (128, own)))
+    dcol[own:2 * own, :] = jnp.transpose(jnp.broadcast_to(dual2[...] * log2e, (128, own)))
     rcopy(tgt, T2, s_pair.at[0], r_pair.at[0], sib).wait_recv()
 
     lane_rep = C // 128
@@ -176,14 +177,14 @@
         for h, t in ((0, tgt), (1, T2)):
             p = lax.dot_general(t[...], block, (((1,), (1,)), ((), ())), preferred_element_type=F32)
             dc = dcol[h * own:(h + 1) * own, :]
-            s = score_scale * p + jnp.concatenate([dc] * lane_rep, axis=1)
+            s = (score_scale * log2e) * p + jnp.concatenate([dc] * lane_rep, axis=1)
             e_buf[g, h * own:(h + 1) * own, :] = s
             tops.append(jnp.max(s, axis=0, keepdims=True))
         top = jnp.maximum(tops[0], tops[1])
         m_buf[g] = top
-        e = jnp.exp(e_buf[g] - top)
+        e = jnp.exp2(e_buf[g] - top)
         e_buf[g] = e
-        lam[g, me] = top + jnp.log(jnp.sum(e, axis=0, keepdims=True))
+        lam[g, me] = top + log2e * jnp.log(jnp.sum(e, axis=0, keepdims=True))
 
     def take(g, r):
         rcopy(S.at[g, r], S.at[g, r], s_x.at[0, 0], r_x.at[r, g], sib).wait_recv()
@@ -222,8 +223,8 @@
         lam_all(g).wait_recv()
         parts = lam[g]
         peak = jnp.max(parts, axis=0)
-        log_total = peak + jnp.log(jnp.sum(jnp.exp(parts - peak[None]), axis=0))
-        return wm_g[g, 0:1, :] * jnp.exp(m_buf[g] - log_total)
+        log_total = peak + log2e * jnp.log(jnp.sum(jnp.exp2(parts - peak[None]), axis=0))
+        return wm_g[g, 0:1, :] * jnp.exp2(m_buf[g] - log_total)
 
     def round_delta(g, h, scale):
         hit = jnp.where(hits(g, h), wm_g[g, 0:1, :], 0.0)
@@ -248,19 +249,19 @@
             uh = lax.dot_general(jnp.where(hit, 0.0, e).astype(BF16), t[...], over_targets, preferred_element_type=F32)
             kh = lax.dot_general(jnp.where(hit, 1.0, 0.0).astype(BF16), t[...], over_targets, preferred_element_type=F32)
             u, k, m = (uh, kh, at) if h == 0 else (u + uh, k + kh, m + at)
-        U[...] = u
-        H[...] = k
-        em[...] = m
+        U[g] = u
+        H[g] = k
+        em[g] = m
 
     def prepared(g):
         scale = scale_of(g)
         m_buf[g] = scale
-        coef = (scale * em[...] - wm_g[g, 0:1, :]).astype(BF16).astype(F32)
+        coef = (scale * em[g] - wm_g[g, 0:1, :]).astype(BF16).astype(F32)
 
         def down(v):
             return jnp.concatenate([jnp.transpose(jnp.broadcast_to(v, (128, C)))] * (D // 128), axis=1)
 
-        return down(scale) * U[...] + down(coef) * H[...]
+        return down(scale) * U[g] + down(coef) * H[g]
 
     def p_send(g, j):
         apart = (grp != g).astype(jnp.int32)
@@ -277,7 +278,9 @@
             acc = q if acc is None else acc + q
         return acc
 
-    prepare(order[0])
+    early = order
+    for g in early:
+        prepare(g)
 
     def taken(g, j):
         rcopy(ps.at[g, rows[j]], px.at[g, rows[j]], s_p.at[j, g], r_p.at[rows[j], g], sib).wait_recv()
@@ -298,7 +301,7 @@
     for i, g in enumerate(order):
         if i == G - 1 and G > 1:
             gt_send[...] = gt_half(1, order[:-1])
-        part = (prepared(g) if i == 0 else delta_chunk(g)).reshape(R, n, D)
+        part = (prepared(g) if g in early else delta_chunk(g)).reshape(R, n, D)
         ps[g] = part.astype(BF16)
         if far:
             far_send(g).start()
@@ -313,7 +316,7 @@
         def _(part=part):
             partf[...] = part
 
-        if i == 0:
+        if g in early:
             for h in range(2):
                 round_delta(g, h, m_buf[g])
 
@@ -416,9 +419,9 @@
             pltpu.VMEM((G, 1, C), F32),
             pltpu.VMEM((G, R * G, 1, C), F32),
             pltpu.VMEM((G, 2 * own, C), BF16),
-            pltpu.VMEM((C, D), F32),
-            pltpu.VMEM((C, D), F32),
-            pltpu.VMEM((1, C), F32),
+            pltpu.VMEM((G, C, D), F32),
+            pltpu.VMEM((G, C, D), F32),
+            pltpu.VMEM((G, 1, C), F32),
             pltpu.VMEM((G, R, n, D), BF16),
             pltpu.VMEM((G, R, n, D), BF16),
             pltpu.VMEM((G, n, D), BF16),

time: 27.4 us -> 26.9 us (0.982)
    pallas_call x1, Pallas kernels: 25.5 us -> 25.2 us  [per_device(): pl.pallas_call(functools.partial(kernel, R, NC, ND), out_shape=(jax.Shape...]
where the time goes in v4:
time: 26.9 us; the launch traced here: 26.7 us
  Pallas kernels  26.1 us (97%)
  between operations  0.64 us (2%)
    pallas_call x1, Pallas kernels, per_device(): pl.pallas_call(functools.partial(kernel, R, NC, ND), out_shape=(jax.Shape...  25.2 us
    pallas_call x1, Pallas kernels, per_device(): pl.pallas_call(flush, out_shape=(jax.ShapeDtypeStruct((n, D), F32), jax.S...  0.82 us

profile of v4, /device:TPU:0, one launch (start us, length us, event | category | flops | bytes accessed | tf_op | source)
XLA Modules:
  0.0 26.7 jit_solution(10605545150101584090)
XLA Ops:
  0.6 25.2 %shard_map.68 = (f32[64,256]{1,0:T(8,128)S(1)}, f32[512,256]{1,0:T(8,128)S(1)}) custom-call(bf16[64,256]{1,0:T(8,128)(2,1)} %src_h.1, bf16[512,256]{1,0:T(8,128)(2,1)} %tgt_h.1, f32[1,2048]{1,0:T(1,128)} %bitcast.3, f32[1,512]{1,0:T(1,128)} %bitcast.4, s32[1,512]{1,0:T(1,128)} %bitcast.5), custom_call_target="tpu_custom_call" | custom-call | tf_op jit(solution)/shard_map/pallas_call | solution.py:398
  25.9 0.8 %shard_map.69 = (f32[64,256]{1,0:T(8,128)}, f32[512,256]{1,0:T(8,128)}) custom-call(f32[64,256]{1,0:T(8,128)S(1)} %get-tuple-element.4.gs, f32[512,256]{1,0:T(8,128)S(1)} %get-tuple-element.5.gt), custom_call_target="tpu_custom_call" | custom-call | tf_op jit(solution)/shard_map/pallas_call | solution.py:454
